TPU v7x, 256 devices: a whole 4x4x8 slice. The times are simulated.
256 devices in a mesh: rows: 32 (over x, z_lo, core), cols: 8 (over y, z_hi).
Axes of the slice: x: 4, y: 4, z: 8 (z_hi: 2, z_lo: 4; z = z_hi * 4 + z_lo), core: 2. Of those that a mesh axis runs over, the one named last changes fastest.
Arguments:
- matrix_blocks: bfloat16 [8192, 64, 1728], P(('rows', 'cols')), may hold values from -0.75 to 0.75
- restrict: bfloat16 [8192, 4096], P(('rows', 'cols')), may hold values from -1.5 to 1.5
- columns: int32 [8192, 27], P(('rows', 'cols')), may hold values from 0 to 767
- counts: int32 [8192], P(('rows', 'cols')), may hold values from 8 to 27, as said below
- aggregate: int32 [8192], P(('rows', 'cols')), may hold values from 0 to 1
Outputs:
- coarse: float32 [512, 64, 3072], P(('rows', 'cols'))
Inputs may be any that keep to these rules, and one draw needn't show every extreme that they name: `counts`: used slots are the first ones of a row; some row uses all 27.
All inputs are finite; a program needn't handle non-finite values.
Results may differ from a plain program's by a relative error of at most 0.0029.
Values may be sent and summed in bfloat16 or wider, within the bound.
A program may use at most 192 MiB of HBM per device.

v0:
```python
import jax
import jax.numpy as jnp
from jax import lax
from jax.sharding import PartitionSpec as P

BLK = 64
SLOTS = 27
ROWS_DEV = 32
AGG_DEV = 2


def padded(block, sides, width):
    for axis, dim in sides:
        count = lax.axis_size(axis)
        forward = [(i, i + 1) for i in range(count - 1)]
        backward = [(target, source) for source, target in forward]
        low = lax.ppermute(
            lax.slice_in_dim(block, block.shape[dim] - width, None, axis=dim), axis, forward
        )
        high = lax.ppermute(lax.slice_in_dim(block, 0, width, axis=dim), axis, backward)
        block = jnp.concatenate([low, block, high], axis=dim)
    return block


def per_device(matrix_blocks, restrict, columns, counts, aggregate):
    col_count = lax.axis_size("cols")
    row_count = lax.axis_size("rows")
    slab_index = lax.axis_index("rows")
    slab_rows = ROWS_DEV * col_count
    window = 3 * AGG_DEV * col_count
    slab_blocks, slab_aggs = (
        lax.all_gather(restrict, "cols", axis=0, tiled=True),
        lax.all_gather(aggregate, "cols", axis=0, tiled=True),
    )
    near_blocks, near_aggs = (
        padded(slab_blocks, (("rows", 0),), slab_rows),
        padded(slab_aggs, (("rows", 0),), slab_rows),
    )
    slot_index = jnp.arange(SLOTS, dtype=jnp.int32)
    inside = ((columns >= slab_rows) | (slab_index > 0)) & (
        (columns < 2 * slab_rows) | (slab_index < row_count - 1)
    )
    live_mask = ((slot_index[None, :] < counts[:, None]) & inside).astype(jnp.float32)
    slot_ids = columns // ROWS_DEV * AGG_DEV + near_aggs[columns]
    segment = aggregate[:, None] * window + slot_ids
    targets = jnp.arange(AGG_DEV * window, dtype=jnp.int32)
    one_hot = (segment[:, :, None] == targets[None, None, :]).astype(jnp.float32) * live_mask[
        :, :, None
    ]
    own_blocks = restrict.reshape(ROWS_DEV, BLK, BLK)
    left_prod = jnp.einsum(
        "ips,isn->ipn", own_blocks, matrix_blocks, preferred_element_type=jnp.float32
    )
    left_prod = left_prod.astype(jnp.bfloat16).reshape(ROWS_DEV, BLK, SLOTS, BLK)
    far_blocks = near_blocks[columns.reshape(-1)].reshape(ROWS_DEV, SLOTS, BLK, BLK)
    products = jnp.einsum(
        "ipks,ikqs->ikpq", left_prod, far_blocks, preferred_element_type=jnp.float32
    )
    summed = jnp.einsum(
        "ikm,ikpq->mpq",
        one_hot,
        products,
        precision=lax.Precision.HIGHEST,
        preferred_element_type=jnp.float32,
    )
    return (
        summed.reshape(AGG_DEV, window, BLK, BLK)
        .transpose(0, 2, 1, 3)
        .reshape(AGG_DEV, BLK, window * BLK)
    )


def solution(mesh):
    return jax.shard_map(
        per_device,
        mesh=mesh,
        in_specs=(
            P(("rows", "cols"), None, None),
            P(("rows", "cols"), None),
            P(("rows", "cols"), None),
            P(("rows", "cols")),
            P(("rows", "cols")),
        ),
        out_specs=P(("rows", "cols"), None, None),
        check_vma=False,
    )
```

profile of v0, /device:TPU:97, one launch (start us, length us, event | category | flops | bytes accessed | tf_op | source)
XLA Modules:
  0.0 337.9 jit_solution(14347546717908960223)
XLA Ops:
  6.5 0.0 all-gather.2.cloned.1.call-start
  6.5 0.7 all-gather.2.cloned.1.call-update
  7.3 74.1 %all-gather.2.cloned.1.call-done = bf16[256,4096]{1,0:T(8,128)(2,1)} async-done(((bf16[32,4096]{1,0:T(8,128)(2,1)}), bf16[256,4096]{1,0:T(8,128)(2,1)}) %all-gather.2.cloned.1.call-update) | async-done | bytes 2097168 | tf_op jit(solution)/shard_map/all_gather | solution.py:32
  81.3 6.3 %collective-permute-start.3 = (bf16[256,4096]{1,0:T(8,128)(2,1)}, bf16[256,4096]{1,0:T(8,128)(2,1)}, u32[]{:S(2)}, u32[]{:S(2)}) collective-permute-start(bf16[256,4096]{1,0:T(8,128)(2,1)} %all-gather.2.cloned.1.call-done), channel_id=1, source_target_pairs={{8,0},{16,8},{24,16},{32,24},{40,32},{48,40},{56,48},{64,56},{72,6... | collective-permute-start | bytes 6291464 | tf_op jit(solution)/shard_map/ppermute | solution.py:20
  87.6 5.5 %collective-permute-start.2 = (bf16[256,4096]{1,0:T(8,128)(2,1)}, bf16[256,4096]{1,0:T(8,128)(2,1)}, u32[]{:S(2)}, u32[]{:S(2)}) collective-permute-start(bf16[256,4096]{1,0:T(8,128)(2,1)} %all-gather.2.cloned.1.call-done), channel_id=1, source_target_pairs={{0,8},{8,16},{16,24},{24,32},{32,40},{40,48},{48,56},{56,64},{64,7... | collective-permute-start | bytes 6291464 | tf_op jit(solution)/shard_map/ppermute | solution.py:17
  93.2 1.3 dynamic-slice
  95.1 0.9 dynamic-update-slice
  95.9 44.7 %all-reduce = s32[256]{0:T(256)S(1)} all-reduce(s32[256]{0:T(256)S(1)} %dynamic-update-slice), channel_id=1, replica_groups=mesh['rows'=32,'cols'=8] {'cols'}, use_global_device_ids=true, to_apply=%add | all-reduce | flops 256 | bytes 2048
  140.6 1.9 collective-permute-start.1
  142.5 6.3 %collective-permute-start = (s32[256]{0:T(256)S(1)}, s32[256]{0:T(256)S(1)}, u32[]{:S(2)}, u32[]{:S(2)}) collective-permute-start(s32[256]{0:T(256)S(1)} %all-reduce), channel_id=1, source_target_pairs={{0,8},{8,16},{16,24},{24,32},{32,40},{40,48},{48,56},{56,64},{64,7... | collective-permute-start | bytes 3080 | tf_op jit(solution)/shard_map/ppermute | solution.py:17
  148.9 1.5 reshape.51
  150.4 0.8 reshape.53
  151.2 0.7 add_select_fusion
  151.9 0.1 reshape.59
  152.1 0.7 broadcast_multiply_fusion
  152.7 0.8 fusion.18
  153.5 8.1 %convolution_convert_fusion = bf16[32,64,1728]{2,1,0:T(8,128)(2,1)} fusion(bf16[32,64,64]{2,1,0:T(8,128)(2,1)S(1)} %reshape.51, bf16[32,64,1728]{2,1,0:T(8,128)(2,1)} %param.5), kind=kOutput, calls=%fused_computation.7 | convolution fusion | flops 456523776 | bytes 14417920 | tf_op jit(solution)/shard_map/ips,isn->ipn/dot_general | solution.py:51
  161.6 22.9 %reshape.52 = bf16[32,64,27,64]{3,2,1,0:T(8,128)(2,1)} reshape(bf16[32,64,1728]{2,1,0:T(8,128)(2,1)} %convolution_convert_fusion) | data formatting | bytes 14155776 | tf_op jit(solution)/shard_map/reshape | solution.py:54
  184.5 0.1 copy.13
  184.6 0.0 collective-permute-done.1
  184.6 0.0 collective-permute-done
  184.6 0.0 copy-start.1
  184.6 0.0 copy-start
  184.7 3.7 %gather_fusion = s32[864]{0:T(1024)S(1)} fusion(s32[768]{0:T(1024)S(1)} %pad_add_fusion, s32[1024]{0:T(1024)S(1)} %pad_clamp_fusion.1), kind=kCustom, calls=%fused_computation | custom fusion | bytes 10368 | tf_op jit(solution)/shard_map/gather | solution.py:44
  188.3 0.1 reshape.58
  188.4 0.0 copy-done.1
  188.4 0.1 fusion.15
  188.5 0.1 copy.12
  188.6 0.0 collective-permute-done.3
  188.6 0.0 collective-permute-done.2
  188.6 0.0 copy-done
  188.6 5.5 %pad_maximum_fusion = bf16[768,4096]{1,0:T(8,128)(2,1)} fusion(bf16[256,4096]{1,0:T(8,128)(2,1)} %collective-permute-done.3, bf16[256,4096]{1,0:T(8,128)(2,1)S(1)} %copy-done, bf16[256,4096]{1,0:T(8,128)(2,1)} %collective-permute-done.2), kind=kLoop, calls=%fused_computation.6 | loop fusion | flops 18874368 | bytes 12582912 | tf_op jit(solution)/shard_map/concatenate | solution.py:21
  194.1 18.5 %gather_fusion.1 = bf16[864,4096]{1,0:T(8,128)(2,1)} fusion(bf16[768,4096]{1,0:T(8,128)(2,1)} %pad_maximum_fusion, s32[1024]{0:T(1024)S(1)} %pad_clamp_fusion), kind=kCustom, calls=%fused_computation.1 | custom fusion | bytes 14159232 | tf_op jit(solution)/shard_map/gather | solution.py:55
  212.6 20.0 %reshape.54 = bf16[32,27,64,64]{3,2,1,0:T(8,128)(2,1)} reshape(bf16[864,4096]{1,0:T(8,128)(2,1)} %gather_fusion.1) | data formatting | bytes 14155776 | tf_op jit(solution)/shard_map/reshape | solution.py:55
  232.5 23.6 %fusion.2 = f32[32,27,64,64]{3,2,1,0:T(8,128)} fusion(bf16[32,27,64,64]{3,2,1,0:T(8,128)(2,1)} %reshape.54, bf16[32,64,27,64]{3,2,1,0:T(8,128)(2,1)} %reshape.52), kind=kOutput, calls=%fused_computation.4 | convolution fusion | flops 452984832 | bytes 28311552 | tf_op jit(solution)/shard_map/ipks,ikqs->ikpq/dot_general | solution.py:56
  256.1 64.2 %fusion.4 = f32[96,64,64]{0,2,1:T(8,128)} fusion(f32[32,27,64,64]{3,2,1,0:T(8,128)} %fusion.2, f32[32,27]{0,1:T(8,128)S(1)} %copy.13, s32[32,27]{0,1:T(8,128)S(1)} %copy.12), kind=kOutput, calls=%fused_computation.8 | convolution fusion | flops 4077029376 | bytes 15735552 | tf_op jit(solution)/shard_map/ikm,ikpq->mpq/dot_general | solution.py:59
  320.3 4.0 %copy.16 = f32[96,64,64]{2,1,0:T(8,128)S(1)} copy(f32[96,64,64]{0,2,1:T(8,128)} %fusion.4) | data formatting | bytes 3145728 | tf_op jit(solution)/shard_map/ikm,ikpq->mpq/dot_general | solution.py:59
  324.3 3.5 %copy.17 = f32[2,64,48,64]{3,2,1,0:T(8,128)} copy(f32[2,64,48,64]{3,1,2,0:T(8,128)S(1)} %bitcast.15) | data formatting | bytes 3145728 | tf_op jit(solution)/shard_map/transpose | solution.py:68
  327.8 3.2 reshape.56
  (5 shorter events, 0.0 us)
Async XLA Ops:
  6.5 74.8 %all-gather.2.cloned.1.call-start = ((), (), s32[]{:S(2)}) async-start(), calls=%async_computation | async-start | bytes 2359296 | tf_op jit(solution)/shard_map/all_gather | solution.py:32
  81.3 107.3 %collective-permute-start.3 = (bf16[256,4096]{1,0:T(8,128)(2,1)}, bf16[256,4096]{1,0:T(8,128)(2,1)}, u32[]{:S(2)}, u32[]{:S(2)}) collective-permute-start(bf16[256,4096]{1,0:T(8,128)(2,1)} %all-gather.2.cloned.1.call-done), channel_id=1, source_target_pairs={{8,0},{16,8},{24,16},{32,24},{40,32},{48,40},{56,48},{64,56},{72,6... | collective-permute-start | bytes 6291464 | tf_op jit(solution)/shard_map/ppermute | solution.py:20
  87.6 101.0 %collective-permute-start.2 = (bf16[256,4096]{1,0:T(8,128)(2,1)}, bf16[256,4096]{1,0:T(8,128)(2,1)}, u32[]{:S(2)}, u32[]{:S(2)}) collective-permute-start(bf16[256,4096]{1,0:T(8,128)(2,1)} %all-gather.2.cloned.1.call-done), channel_id=1, source_target_pairs={{0,8},{8,16},{16,24},{24,32},{32,40},{40,48},{48,56},{56,64},{64,7... | collective-permute-start | bytes 6291464 | tf_op jit(solution)/shard_map/ppermute | solution.py:17
  140.6 44.0 %collective-permute-start.1 = (s32[256]{0:T(256)S(1)}, s32[256]{0:T(256)S(1)}, u32[]{:S(2)}, u32[]{:S(2)}) collective-permute-start(s32[256]{0:T(256)S(1)} %all-reduce), channel_id=1, source_target_pairs={{8,0},{16,8},{24,16},{32,24},{40,32},{48,40},{56,48},{64,56},{72,6... | collective-permute-start | bytes 3080 | tf_op jit(solution)/shard_map/ppermute | solution.py:20
  142.5 42.1 %collective-permute-start = (s32[256]{0:T(256)S(1)}, s32[256]{0:T(256)S(1)}, u32[]{:S(2)}, u32[]{:S(2)}) collective-permute-start(s32[256]{0:T(256)S(1)} %all-reduce), channel_id=1, source_target_pairs={{0,8},{8,16},{16,24},{24,32},{32,40},{40,48},{48,56},{56,64},{64,7... | collective-permute-start | bytes 3080 | tf_op jit(solution)/shard_map/ppermute | solution.py:17
  184.6 3.8 %copy-start.1 = (s32[32,27]{1,0:T(8,128)S(1)}, s32[32,27]{1,0:T(8,128)}, u32[]{:S(2)}) copy-start(s32[32,27]{1,0:T(8,128)} %param.7) | copy-start | bytes 10372
  184.6 4.0 %copy-start = (bf16[256,4096]{1,0:T(8,128)(2,1)S(1)}, bf16[256,4096]{1,0:T(8,128)(2,1)}, u32[]{:S(2)}) copy-start(bf16[256,4096]{1,0:T(8,128)(2,1)} %all-gather.2.cloned.1.call-done) | copy-start | bytes 6291460
Sparse Core Ops, SparseCore 0:
  10.0 71.3 all-gather.1
where the time goes:
time: 339 us; the launch traced here: 338 us
  matrix products  95.9 us (28%)
  local copies, waits for them, and re-layouts  80.5 us (24%)
  waiting for transfers between devices  74.8 us (22%)
  blocking collectives  44.7 us (13%)
  starting transfers between devices  20.1 us (6%)
  between operations  14.2 us (4%)
  other arithmetic  7.74 us (2%)
    all_gather x1, waiting for transfers between devices, per_device(): lax.all_gather(restrict, 'cols', axis=0, tiled=True)  74.1 us
    dot_general x1, matrix products, per_device(): jnp.einsum('ikm,ikpq->mpq', one_hot, products, precision=lax.Precision.HI...  64.2 us
    unnamed x1, blocking collectives  44.7 us
    dot_general x1, matrix products, per_device(): jnp.einsum('ipks,ikqs->ikpq', left_prod, far_blocks, preferred_element_ty...  23.6 us
    reshape x1, local copies, waits for them, and re-layouts, per_device(): left_prod.astype(jnp.bfloat16).reshape(ROWS_DEV, BLK, SLOTS, BLK)  22.9 us
    reshape x1, local copies, waits for them, and re-layouts, per_device(): near_blocks[columns.reshape(-1)].reshape(ROWS_DEV, SLOTS, BLK, BLK)  20 us
    gather x1, local copies, waits for them, and re-layouts, per_device(): near_blocks[columns.reshape(-1)].reshape(ROWS_DEV, SLOTS, BLK, BLK)  18.5 us
    ppermute x2, starting transfers between devices, padded(): lax.ppermute(lax.slice_in_dim(block, block.shape[dim] - width, None, axis...  11.8 us
  transfers between devices with their start and end apart: 5, of which 1 were waited for; matrix products, arithmetic and copies ran while one was open for 12% of the time, Pallas kernels for 0%

commit v1 on v0

--- a/solution.py
+++ b/solution.py
@@ -29,7 +29,9 @@
     slab_rows = ROWS_DEV * col_count
     window = 3 * AGG_DEV * col_count
     slab_blocks, slab_aggs = (
-        lax.all_gather(restrict, "cols", axis=0, tiled=True),
+        jnp.concatenate(
+            lax.all_to_all(jnp.stack([restrict] * lax.axis_size("cols")), "cols", 0, 0), axis=0
+        ),
         lax.all_gather(aggregate, "cols", axis=0, tiled=True),
     )
     near_blocks, near_aggs = (

time: 339 us -> 305 us (0.90)
  the two profiles are of different devices: /device:TPU:97 before, /device:TPU:229 now
where the time goes in v1:
time: 305 us; the launch traced here: 304 us
  matrix products  95.9 us (31%)
  blocking collectives  93.5 us (31%)
  local copies, waits for them, and re-layouts  81 us (27%)
  starting transfers between devices  26.9 us (9%)
  other arithmetic  5.66 us (2%)
    dot_general x1, matrix products, per_device(): jnp.einsum('ikm,ikpq->mpq', one_hot, products, precision=lax.Precision.HI...  64.2 us
    unnamed x1, blocking collectives  54 us
    all_to_all x1, blocking collectives, per_device(): lax.all_to_all(jnp.stack([restrict] * lax.axis_size('cols')), 'cols', 0, 0)  39.5 us
    dot_general x1, matrix products, per_device(): jnp.einsum('ipks,ikqs->ikpq', left_prod, far_blocks, preferred_element_ty...  23.6 us
    reshape x1, local copies, waits for them, and re-layouts, per_device(): left_prod.astype(jnp.bfloat16).reshape(ROWS_DEV, BLK, SLOTS, BLK)  22.9 us
    reshape x1, local copies, waits for them, and re-layouts, per_device(): near_blocks[columns.reshape(-1)].reshape(ROWS_DEV, SLOTS, BLK, BLK)  20 us
    ppermute x2, starting transfers between devices, padded(): lax.ppermute(lax.slice_in_dim(block, 0, width, axis=dim), axis, backward)  18.7 us
    gather x1, local copies, waits for them, and re-layouts, per_device(): near_blocks[columns.reshape(-1)].reshape(ROWS_DEV, SLOTS, BLK, BLK)  18.5 us
  transfers between devices with their start and end apart: 4, of which 0 were waited for; matrix products, arithmetic and copies ran while one was open for 13% of the time, Pallas kernels for 0%

profile of v1, /device:TPU:229, one launch (start us, length us, event | category | flops | bytes accessed | tf_op | source)
XLA Modules:
  0.0 303.8 jit_solution(14577961655146375104)
XLA Ops:
  0.0 0.0 copy-start.2
  0.0 0.0 copy-start
  0.0 0.0 copy-start.1
  0.0 1.2 stack.2
  1.2 39.5 %all_to_all.5 = bf16[8,32,4096]{2,1,0:T(8,128)(2,1)S(1)} all-to-all(bf16[8,32,4096]{2,1,0:T(8,128)(2,1)S(1)} %stack.2), channel_id=1, replica_groups=mesh['rows'=32,'cols'=8] {'cols'}, dimensions={0} | all-to-all | bytes 4194304 | tf_op jit(solution)/shard_map/all_to_all | solution.py:33
  40.7 16.8 %collective-permute-start.3 = (bf16[256,4096]{1,0:T(8,128)(2,1)S(1)}, bf16[256,4096]{1,0:T(8,128)(2,1)}, u32[]{:S(2)}, u32[]{:S(2)}) collective-permute-start(bf16[256,4096]{1,0:T(8,128)(2,1)S(1)} %bitcast.17), channel_id=1, source_target_pairs={{8,0},{16,8},{24,16},{32,24},{40,32},{48,40},{56,48},{64,56},{72,6... | collective-permute-start | bytes 6291464 | tf_op jit(solution)/shard_map/ppermute | solution.py:20
  57.5 1.9 collective-permute-start.2
  59.4 1.3 dynamic-slice
  61.3 0.9 dynamic-update-slice
  62.2 54.0 %all-reduce = s32[256]{0:T(256)S(1)} all-reduce(s32[256]{0:T(256)S(1)} %dynamic-update-slice), channel_id=1, replica_groups=mesh['rows'=32,'cols'=8] {'cols'}, use_global_device_ids=true, to_apply=%add | all-reduce | flops 256 | bytes 2048
  116.2 1.9 collective-permute-start.1
  118.1 6.3 %collective-permute-start = (s32[256]{0:T(256)S(1)}, s32[256]{0:T(256)S(1)}, u32[]{:S(2)}, u32[]{:S(2)}) collective-permute-start(s32[256]{0:T(256)S(1)} %all-reduce), channel_id=1, source_target_pairs={{0,8},{8,16},{16,24},{24,32},{32,40},{40,48},{48,56},{56,64},{64,7... | collective-permute-start | bytes 3080 | tf_op jit(solution)/shard_map/ppermute | solution.py:17
  124.5 1.5 reshape.56
  125.9 0.0 copy-done
  125.9 0.1 reshape.59
  126.1 0.1 reshape.65
  126.2 0.0 copy-done.2
  126.2 0.0 copy-done.1
  126.2 0.1 fusion.18
  126.3 8.1 %convolution_convert_fusion = bf16[32,64,1728]{2,1,0:T(8,128)(2,1)} fusion(bf16[32,64,64]{2,1,0:T(8,128)(2,1)S(1)} %reshape.56, bf16[32,64,1728]{2,1,0:T(8,128)(2,1)} %param.5), kind=kOutput, calls=%fused_computation.7 | convolution fusion | flops 456523776 | bytes 14417920 | tf_op jit(solution)/shard_map/ips,isn->ipn/dot_general | solution.py:53
  134.4 22.9 %reshape.57 = bf16[32,64,27,64]{3,2,1,0:T(8,128)(2,1)} reshape(bf16[32,64,1728]{2,1,0:T(8,128)(2,1)} %convolution_convert_fusion) | data formatting | bytes 14155776 | tf_op jit(solution)/shard_map/reshape | solution.py:56
  157.4 0.1 copy.13
  157.4 0.0 collective-permute-done.1
  157.4 0.0 collective-permute-done
  157.5 3.7 %gather_fusion = s32[864]{0:T(1024)S(1)} fusion(s32[768]{0:T(1024)S(1)} %pad_add_fusion, s32[1024]{0:T(1024)S(1)} %pad_clamp_fusion.1), kind=kCustom, calls=%fused_computation | custom fusion | bytes 10368 | tf_op jit(solution)/shard_map/gather | solution.py:46
  161.1 0.1 reshape.64
  161.2 0.1 fusion.15
  161.3 0.1 copy.12
  161.4 0.0 collective-permute-done.3
  161.4 0.0 collective-permute-done.2
  161.4 5.5 %pad_maximum_fusion = bf16[768,4096]{1,0:T(8,128)(2,1)} fusion(bf16[256,4096]{1,0:T(8,128)(2,1)} %collective-permute-done.3, bf16[256,4096]{1,0:T(8,128)(2,1)S(1)} %bitcast.19, bf16[256,4096]{1,0:T(8,128)(2,1)} %collective-permute-done.2), kind=kLoop, calls=%fused_computation.6 | loop fusion | flops 18874368 | bytes 12582912 | tf_op jit(solution)/shard_map/concatenate | solution.py:21
  166.9 18.5 %gather_fusion.1 = bf16[864,4096]{1,0:T(8,128)(2,1)} fusion(bf16[768,4096]{1,0:T(8,128)(2,1)} %pad_maximum_fusion, s32[1024]{0:T(1024)S(1)} %pad_clamp_fusion), kind=kCustom, calls=%fused_computation.1 | custom fusion | bytes 14159232 | tf_op jit(solution)/shard_map/gather | solution.py:57
  185.3 20.0 %reshape.60 = bf16[32,27,64,64]{3,2,1,0:T(8,128)(2,1)} reshape(bf16[864,4096]{1,0:T(8,128)(2,1)} %gather_fusion.1) | data formatting | bytes 14155776 | tf_op jit(solution)/shard_map/reshape | solution.py:57
  205.3 23.6 %fusion.2 = f32[32,27,64,64]{3,2,1,0:T(8,128)} fusion(bf16[32,27,64,64]{3,2,1,0:T(8,128)(2,1)} %reshape.60, bf16[32,64,27,64]{3,2,1,0:T(8,128)(2,1)} %reshape.57), kind=kOutput, calls=%fused_computation.4 | convolution fusion | flops 452984832 | bytes 28311552 | tf_op jit(solution)/shard_map/ipks,ikqs->ikpq/dot_general | solution.py:58
  228.9 64.2 %fusion.4 = f32[96,64,64]{0,2,1:T(8,128)} fusion(f32[32,27,64,64]{3,2,1,0:T(8,128)} %fusion.2, f32[32,27]{0,1:T(8,128)S(1)} %copy.13, s32[32,27]{0,1:T(8,128)S(1)} %copy.12), kind=kOutput, calls=%fused_computation.8 | convolution fusion | flops 4077029376 | bytes 15735552 | tf_op jit(solution)/shard_map/ikm,ikpq->mpq/dot_general | solution.py:61
  293.1 4.0 %copy.16 = f32[96,64,64]{2,1,0:T(8,128)S(1)} copy(f32[96,64,64]{0,2,1:T(8,128)} %fusion.4) | data formatting | bytes 3145728 | tf_op jit(solution)/shard_map/ikm,ikpq->mpq/dot_general | solution.py:61
  297.1 3.5 %copy.17 = f32[2,64,48,64]{3,2,1,0:T(8,128)} copy(f32[2,64,48,64]{3,1,2,0:T(8,128)S(1)} %bitcast.16) | data formatting | bytes 3145728 | tf_op jit(solution)/shard_map/transpose | solution.py:70
  300.6 3.2 %reshape.62 = f32[2,64,3072]{2,1,0:T(8,128)} reshape(f32[2,64,48,64]{3,2,1,0:T(8,128)} %copy.17) | data formatting | bytes 3145728 | tf_op jit(solution)/shard_map/reshape | solution.py:71
  (7 shorter events, 0.0 us)
Async XLA Ops:
  0.0 126.2 %copy-start.2 = (s32[32]{0:T(128)S(1)}, s32[32]{0:T(128)}, u32[]{:S(2)}) copy-start(s32[32]{0:T(128)} %param.9) | copy-start | bytes 388
  0.0 125.9 %copy-start = (s32[32,27]{1,0:T(8,128)S(1)}, s32[32,27]{1,0:T(8,128)}, u32[]{:S(2)}) copy-start(s32[32,27]{1,0:T(8,128)} %param.7) | copy-start | bytes 10372
  0.0 126.2 %copy-start.1 = (s32[32]{0:T(128)S(1)}, s32[32]{0:T(128)}, u32[]{:S(2)}) copy-start(s32[32]{0:T(128)} %param.8) | copy-start | bytes 388
  40.7 120.7 %collective-permute-start.3 = (bf16[256,4096]{1,0:T(8,128)(2,1)S(1)}, bf16[256,4096]{1,0:T(8,128)(2,1)}, u32[]{:S(2)}, u32[]{:S(2)}) collective-permute-start(bf16[256,4096]{1,0:T(8,128)(2,1)S(1)} %bitcast.17), channel_id=1, source_target_pairs={{8,0},{16,8},{24,16},{32,24},{40,32},{48,40},{56,48},{64,56},{72,6... | collective-permute-start | bytes 6291464 | tf_op jit(solution)/shard_map/ppermute | solution.py:20
  57.5 103.9 %collective-permute-start.2 = (bf16[256,4096]{1,0:T(8,128)(2,1)S(1)}, bf16[256,4096]{1,0:T(8,128)(2,1)}, u32[]{:S(2)}, u32[]{:S(2)}) collective-permute-start(bf16[256,4096]{1,0:T(8,128)(2,1)S(1)} %bitcast.18), channel_id=1, source_target_pairs={{0,8},{8,16},{16,24},{24,32},{32,40},{40,48},{48,56},{56,64},{64,7... | collective-permute-start | bytes 6291464 | tf_op jit(solution)/shard_map/ppermute | solution.py:17
  116.2 41.3 %collective-permute-start.1 = (s32[256]{0:T(256)S(1)}, s32[256]{0:T(256)S(1)}, u32[]{:S(2)}, u32[]{:S(2)}) collective-permute-start(s32[256]{0:T(256)S(1)} %all-reduce), channel_id=1, source_target_pairs={{8,0},{16,8},{24,16},{32,24},{40,32},{48,40},{56,48},{64,56},{72,6... | collective-permute-start | bytes 3080 | tf_op jit(solution)/shard_map/ppermute | solution.py:20
  118.1 39.3 %collective-permute-start = (s32[256]{0:T(256)S(1)}, s32[256]{0:T(256)S(1)}, u32[]{:S(2)}, u32[]{:S(2)}) collective-permute-start(s32[256]{0:T(256)S(1)} %all-reduce), channel_id=1, source_target_pairs={{0,8},{8,16},{16,24},{24,32},{32,40},{40,48},{48,56},{56,64},{64,7... | collective-permute-start | bytes 3080 | tf_op jit(solution)/shard_map/ppermute | solution.py:17
